TPU v7x, 32 devices: a whole 2x2x4 slice. The times are simulated.
32 devices in a mesh: users: 16 (over z, y, core), heads: 2 (over x).
Axes of the slice: x: 2, y: 2, z: 4, core: 2. Of those that a mesh axis runs over, the one named last changes fastest.
Arguments:
- sessions: bfloat16 [8192, 4096], P(('users', 'heads')), parts along dimension 0, may hold values from -16 to 16
- input_weight: bfloat16 [3, 4096, 2048], P(None, None, 'heads'), may hold values from -1 to 1
- output_weight: bfloat16 [2048, 4096], P('heads'), may hold values from -0.359375 to 0.359375
- session_counts: int32 [32], P('users'), parts along dimension 0, may hold values from 1 to 384, 512 in all
Outputs:
- attended: bfloat16 [8192, 4096], P(('users', 'heads')), parts along dimension 0
There are 16 independent parts, one for each index of `users`. A program takes and returns all parts, laid end to end along the dimension named above; an argument that names none is the same for every part. Nothing has to cross between parts.
Inputs may be any that keep to these rules, and one draw needn't show every extreme that they name: `session_counts`: the 2 counts sum to 512.
All inputs are finite; a program needn't handle non-finite values.
Results may differ from a plain program's by a relative error of at most 0.015.
Values may be sent and summed in bfloat16 or wider, within the bound.
No kernel may reach another device: no remote copies, remote signals or barrier semaphores. Data moves between devices by JAX's collectives and lax.ppermute only.
A program may use at most 128 MiB of HBM per device.

v0:
```python
import jax
import jax.numpy as jnp
from jax import lax
from jax.sharding import PartitionSpec as P

HD = 128


def permitted(total, counts):
    positions = jnp.arange(total, dtype=jnp.int32)
    ends = jnp.cumsum(counts)
    row_user = jnp.sum((positions[:, None] >= ends[None, :]).astype(jnp.int32), axis=1)
    same_user = row_user[:, None] == row_user[None, :]
    return jnp.logical_and(same_user, positions[:, None] >= positions[None, :])


def attend(packed, allowed):
    total = packed.shape[1]
    width = packed.shape[2]
    block = min(512, total)
    count = total // block
    queries = packed[0].reshape(count, block, width // HD, HD)
    key_rows = packed[1].reshape(total, width // HD, HD)
    values = packed[2].reshape(total, width // HD, HD)
    masks = allowed.reshape(count, block, total)

    def one_block(pair):
        query_block, mask_block = pair
        scores = jnp.einsum(
            "qhe,khe->hqk", query_block, key_rows, preferred_element_type=jnp.float32
        ) * HD ** (-0.5)
        scores = jnp.where(mask_block[None], scores, -1e30)
        highest = jnp.max(scores, axis=2, keepdims=True)
        raised = jnp.where(mask_block[None], jnp.exp(scores - highest), 0.0)
        attn_probs = (raised / jnp.sum(raised, axis=2, keepdims=True)).astype(jnp.bfloat16)
        mixed = jnp.einsum("hqk,khe->qhe", attn_probs, values, preferred_element_type=jnp.float32)
        return mixed.astype(jnp.bfloat16).reshape(block, width)

    blocks_out = lax.map(one_block, (queries, masks))
    return blocks_out.reshape(total, width)


def per_device(sessions, input_weight, output_weight, session_counts):
    packed = jnp.einsum(
        "nd,cde->cne",
        lax.all_gather(sessions, "heads", axis=0, tiled=True),
        input_weight,
        preferred_element_type=jnp.float32,
    ).astype(jnp.bfloat16)
    total = packed.shape[1]
    allowed = permitted(total, session_counts)
    mixed = attend(packed, allowed)
    return lax.psum_scatter(
        jnp.dot(mixed, output_weight, preferred_element_type=jnp.float32).astype(jnp.bfloat16),
        "heads",
        scatter_dimension=0,
        tiled=True,
    )


def solution(mesh):
    in_specs = (P(("users", "heads"), None), P(None, None, "heads"), P("heads", None), P("users"))
    out_specs = P(("users", "heads"), None)
    return jax.shard_map(
        per_device, mesh=mesh, in_specs=in_specs, out_specs=out_specs, check_vma=False
    )
```

profile of v0, /device:TPU:0, one launch (start us, length us, event | category | flops | bytes accessed | tf_op | source)
XLA Modules:
  0.0 167.7 jit_solution(7120729407783168606)
XLA Ops:
  6.5 0.0 all-gather.2.cloned.1.call-start
  6.5 0.7 all-gather.2.cloned.1.call-update
  7.3 0.0 reduce-scatter.2.cloned.1.call-start
  7.3 0.8 reduce-window.8
  8.1 0.1 fusion.14
  8.2 0.2 fusion.11
  8.4 59.9 %all-gather.2.cloned.1.call-done = bf16[512,4096]{1,0:T(8,128)(2,1)} async-done(((bf16[256,4096]{1,0:T(8,128)(2,1)}), bf16[512,4096]{1,0:T(8,128)(2,1)}) %all-gather.2.cloned.1.call-update) | async-done | bytes 4194320 | tf_op jit(solution)/shard_map/all_gather | solution.py:46
  68.4 18.2 %convert_bitcast_fusion = bf16[3,512,1024]{1,2,0:T(8,128)(2,1)S(1)} fusion(bf16[3,4096,1024]{2,1,0:T(8,128)(2,1)} %param.5, bf16[512,4096]{1,0:T(8,128)(2,1)} %all-gather.2.cloned.1.call-done), kind=kOutput, calls=%fused_computation.12 | convolution fusion | flops 12886474752 | bytes 32505856 | tf_op jit(solution)/shard_map/nd,cde->cne/dot_general | solution.py:44
  86.6 0.2 fusion.17
  86.8 5.9 %fusion.18 = (f32[8,512]{1,0:T(8,128)S(1)}, f32[8,512,512]{1,2,0:T(8,128)}) fusion(pred[512,512]{0,1:T(8,128)(4,1)S(1)} %fusion.11, bf16[512,8,128]{0,2,1:T(8,128)(2,1)S(1)} %bitcast.25, bf16[512,8,128]{0,2,1:T(8,128)(2,1)S(1)} %bitcast.24), kind=kOutput, calls=%fused_computation.22 | convolution fusion | flops 547357184 | bytes 10764288 | tf_op jit(solution)/shard_map/while/body/eval_jaxpr/sub | solution.py:34
  92.7 4.1 %fusion.10 = bf16[8,128,512]{2,1,0:T(8,128)(2,1)S(1)} fusion(bf16[512,8,128]{0,2,1:T(8,128)(2,1)S(1)} %bitcast.23, f32[8,512,512]{1,2,0:T(8,128)} %get-tuple-element.26, f32[8,512]{1,0:T(8,128)S(1)} %get-tuple-element.24), kind=kOutput, calls=%fused_computation.13 | convolution fusion | flops 541589504 | bytes 10502144 | tf_op jit(solution)/shard_map/while/body/eval_jaxpr/hqk,khe->qhe/dot_general | solution.py:36
  96.8 9.5 %convolution_convert_fusion = bf16[512,4096]{1,0:T(8,128)(2,1)} fusion(bf16[512,1024]{0,1:T(8,128)(2,1)S(1)} %bitcast.28, bf16[1024,4096]{1,0:T(8,128)(2,1)} %param.6), kind=kOutput, calls=%fused_computation.5 | convolution fusion | flops 4297064448 | bytes 13631488 | tf_op jit(solution)/shard_map/dot_general | solution.py:54
  106.3 0.0 reduce-scatter.2.cloned.1.call-update
  106.4 54.5 %reduce-scatter.2.cloned.1.call-done = bf16[256,4096]{1,0:T(8,128)(2,1)} async-done(((bf16[512,4096]{1,0:T(8,128)(2,1)}), bf16[256,4096]{1,0:T(8,128)(2,1)}) %reduce-scatter.2.cloned.1.call-update) | async-done | bytes 2097168 | tf_op jit(solution)/shard_map/reduce_scatter | solution.py:53
Async XLA Ops:
  6.5 61.8 %all-gather.2.cloned.1.call-start = ((), (), s32[]{:S(2)}) async-start(), calls=%async_computation.1 | async-start | bytes 6291456 | tf_op jit(solution)/shard_map/all_gather | solution.py:46
  7.3 153.6 %reduce-scatter.2.cloned.1.call-start = ((), (), s32[]{:S(2)}) async-start(), calls=%async_computation.2 | async-start | bytes 6291456 | tf_op jit(solution)/shard_map/reduce_scatter | solution.py:53
Sparse Core Ops, SparseCore 0:
  8.9 59.4 all-gather.1
  106.5 54.3 reduce-scatter.1
where the time goes:
time: 168 us
  waiting for transfers between devices  115 us (68%)
  matrix products  37.8 us (22%)
  between operations  13.4 us (8%)
    all_gather x1, waiting for transfers between devices, per_device(): lax.all_gather(sessions, 'heads', axis=0, tiled=True)  59.9 us
    reduce_scatter x1, waiting for transfers between devices, per_device(): lax.psum_scatter(jnp.dot(mixed, output_weight, preferred_element_type=jnp...  54.5 us
    dot_general x1, matrix products, per_device(): jnp.einsum('nd,cde->cne', lax.all_gather(sessions, 'heads', axis=0, tiled...  18.2 us
    dot_general x1, matrix products, per_device(): jnp.dot(mixed, output_weight, preferred_element_type=jnp.float32)  9.48 us
    sub x1, matrix products, one_block(): raised = jnp.where(mask_block[None], jnp.exp(scores - highest), 0.0)  5.92 us
    dot_general x1, matrix products, one_block(): jnp.einsum('hqk,khe->qhe', attn_probs, values, preferred_element_type=jnp...  4.11 us
  transfers between devices with their start and end apart: 2, of which 2 were waited for; matrix products, arithmetic and copies ran while one was open for 1% of the time, Pallas kernels for 0%

commit v1 on v0

--- a/solution.py
+++ b/solution.py
@@ -4,6 +4,30 @@
 from jax.sharding import PartitionSpec as P
 
 HD = 128
+
+
+def shifts_all_put(x0, shard_in):
+    y2 = lax.axis_size("heads")
+    raw_out = lax.axis_index("heads")
+    front, mixed_arr, oldest = (y2, raw_out, x0.shape[0])
+    shelf = [(nth, (nth + 1) % front) for nth in range(front)]
+    block_next, current_block = (x0, None)
+    for j in range(front):
+        reply = (mixed_arr - j) % front
+        local_out = (
+            lax.ppermute(block_next, axis_name="heads", perm=shelf) if j < front - 1 else None
+        )
+        high = shard_in(block_next, reply * oldest)
+        finding = high.shape[1]
+        if current_block is None:
+            current_block = jnp.zeros(
+                (*high.shape[:1], front * finding, *high.shape[2:]), high.dtype
+            )
+        current_block = lax.dynamic_update_slice_in_dim(
+            current_block, high, reply * finding, axis=1
+        )
+        block_next = local_out
+    return current_block
 
 
 def permitted(total, counts):
@@ -41,11 +65,11 @@
 
 
 def per_device(sessions, input_weight, output_weight, session_counts):
-    packed = jnp.einsum(
-        "nd,cde->cne",
-        lax.all_gather(sessions, "heads", axis=0, tiled=True),
-        input_weight,
-        preferred_element_type=jnp.float32,
+    packed = shifts_all_put(
+        sessions,
+        lambda part, at: jnp.einsum(
+            "nd,cde->cne", part, input_weight, preferred_element_type=jnp.float32
+        ),
     ).astype(jnp.bfloat16)
     total = packed.shape[1]
     allowed = permitted(total, session_counts)

time: 168 us -> 150 us (0.89)
  waiting for transfers between devices: 115 us -> 88.2 us
  matrix products: 37.8 us -> 44.1 us
  starting transfers between devices: 0.04 us -> 2.97 us
    all_gather x1 -> x0, waiting for transfers between devices: 59.9 us -> none  [per_device(): lax.all_gather(sessions, 'heads', axis=0, tiled=True)]
    ppermute x0 -> x1, waiting for transfers between devices: none -> 32.2 us  [shifts_all_put(): lax.ppermute(block_next, axis_name='heads', perm=shelf)]
    dot_general x1 -> x2, matrix products: 18.2 us -> 24.5 us  [per_device(): jnp.einsum('nd,cde->cne', part, input_weight, preferred_element_type=jnp....]
    ppermute x0 -> x1, starting transfers between devices: none -> 2.97 us  [shifts_all_put(): lax.ppermute(block_next, axis_name='heads', perm=shelf)]
  transfers between devices with their start and end apart: 2 -> 2, of which waited for: 2 -> 2; matrix products, arithmetic and copies ran while one was open for 1% -> 9% of each run, Pallas kernels for 0% -> 0%
where the time goes in v1:
time: 150 us
  waiting for transfers between devices  88.2 us (59%)
  matrix products  44.1 us (29%)
  between operations  13.4 us (9%)
  starting transfers between devices  2.97 us (2%)
    reduce_scatter x1, waiting for transfers between devices, per_device(): lax.psum_scatter(jnp.dot(mixed, output_weight, preferred_element_type=jnp...  56 us
    ppermute x1, waiting for transfers between devices, shifts_all_put(): lax.ppermute(block_next, axis_name='heads', perm=shelf)  32.2 us
    dot_general x2, matrix products, per_device(): jnp.einsum('nd,cde->cne', part, input_weight, preferred_element_type=jnp....  24.5 us
    dot_general x1, matrix products, per_device(): jnp.dot(mixed, output_weight, preferred_element_type=jnp.float32)  9.48 us
    sub x1, matrix products, one_block(): raised = jnp.where(mask_block[None], jnp.exp(scores - highest), 0.0)  5.92 us
    dot_general x1, matrix products, one_block(): jnp.einsum('hqk,khe->qhe', attn_probs, values, preferred_element_type=jnp...  4.11 us
  transfers between devices with their start and end apart: 2, of which 2 were waited for; matrix products, arithmetic and copies ran while one was open for 9% of the time, Pallas kernels for 0%

profile of v1, /device:TPU:0, one launch (start us, length us, event | category | flops | bytes accessed | tf_op | source)
XLA Modules:
  0.0 150.3 jit_solution(16657075340059103853)
XLA Ops:
  6.5 0.0 reduce-scatter.2.cloned.1.call-start
  6.5 3.0 %collective-permute-start = (bf16[256,4096]{1,0:T(8,128)(2,1)}, bf16[256,4096]{1,0:T(8,128)(2,1)S(1)}, u32[]{:S(2)}, u32[]{:S(2)}) collective-permute-start(bf16[256,4096]{1,0:T(8,128)(2,1)} %param.4), channel_id=1, source_target_pairs={{0,1},{1,0},{2,3},{3,2},{4,5},{5,4},{6,7},{7,6},{8,9},{9,8},{10,11... | collective-permute-start | bytes 6291464 | tf_op jit(solution)/shard_map/ppermute | solution.py:18
  9.5 0.8 reduce-window.8
  10.3 0.1 fusion.18
  10.4 0.2 fusion.15
  10.6 0.2 broadcast_in_dim.42
  10.9 12.3 %bitcast_dynamic-update-slice_fusion.1 = bf16[3,512,1024]{1,2,0:T(8,128)(2,1)S(1)} fusion(bf16[3,512,1024]{1,2,0:T(8,128)(2,1)S(1)} %broadcast_in_dim.42, s32[]{:T(128)S(6)} %select_n.27, bf16[3,4096,1024]{2,1,0:T(8,128)(2,1)} %param.5, bf16[256,4096]{1,0:T(8,128)(2,1)} %param.4), kind=kOutput, calls=%fused_computation.11 | convolution fusion | flops 6442450944 | bytes 30408708 | tf_op jit(solution)/shard_map/nd,cde->cne/dot_general | solution.py:70
  23.2 32.2 %collective-permute-done = bf16[256,4096]{1,0:T(8,128)(2,1)S(1)} collective-permute-done((bf16[256,4096]{1,0:T(8,128)(2,1)}, bf16[256,4096]{1,0:T(8,128)(2,1)S(1)}, u32[]{:S(2)}, u32[]{:S(2)}) %collective-permute-start) | collective-permute-done | bytes 2097184 | tf_op jit(solution)/shard_map/ppermute | solution.py:18
  55.3 12.3 %bitcast_dynamic-update-slice_fusion = bf16[3,512,1024]{1,2,0:T(8,128)(2,1)S(1)} fusion(bf16[3,512,1024]{1,2,0:T(8,128)(2,1)S(1)} %bitcast_dynamic-update-slice_fusion.1, s32[]{:T(128)S(6)} %select_n.29, bf16[3,4096,1024]{2,1,0:T(8,128)(2,1)} %param.5, bf16[256,4096]{1,0:T(8,128)(2,1)S(1)} %collective-permute-done), kind=kOutput, calls=%fused_computation.10 | convolution fusion | flops 6442450944 | bytes 30408708 | tf_op jit(solution)/shard_map/nd,cde->cne/dot_general | solution.py:70
  67.6 0.3 fusion.21
  67.9 5.9 %fusion.22 = (f32[8,512]{1,0:T(8,128)S(1)}, f32[8,512,512]{1,2,0:T(8,128)}) fusion(pred[512,512]{0,1:T(8,128)(4,1)S(1)} %fusion.15, bf16[512,8,128]{0,2,1:T(8,128)(2,1)S(1)} %bitcast.33, bf16[512,8,128]{0,2,1:T(8,128)(2,1)S(1)} %bitcast.32), kind=kOutput, calls=%fused_computation.25 | convolution fusion | flops 547357184 | bytes 10764288 | tf_op jit(solution)/shard_map/while/body/eval_jaxpr/sub | solution.py:58
  73.8 4.1 %fusion.14 = bf16[8,128,512]{2,1,0:T(8,128)(2,1)S(1)} fusion(bf16[512,8,128]{0,2,1:T(8,128)(2,1)S(1)} %bitcast.31, f32[8,512,512]{1,2,0:T(8,128)} %get-tuple-element.26, f32[8,512]{1,0:T(8,128)S(1)} %get-tuple-element.24), kind=kOutput, calls=%fused_computation.16 | convolution fusion | flops 541589504 | bytes 10502144 | tf_op jit(solution)/shard_map/while/body/eval_jaxpr/hqk,khe->qhe/dot_general | solution.py:60
  77.9 9.5 %convolution_convert_fusion = bf16[512,4096]{1,0:T(8,128)(2,1)} fusion(bf16[512,1024]{0,1:T(8,128)(2,1)S(1)} %bitcast.36, bf16[1024,4096]{1,0:T(8,128)(2,1)} %param.6), kind=kOutput, calls=%fused_computation.5 | convolution fusion | flops 4297064448 | bytes 13631488 | tf_op jit(solution)/shard_map/dot_general | solution.py:78
  87.4 0.0 reduce-scatter.2.cloned.1.call-update
  87.4 56.0 %reduce-scatter.2.cloned.1.call-done = bf16[256,4096]{1,0:T(8,128)(2,1)} async-done(((bf16[512,4096]{1,0:T(8,128)(2,1)}), bf16[256,4096]{1,0:T(8,128)(2,1)}) %reduce-scatter.2.cloned.1.call-update) | async-done | bytes 2097168 | tf_op jit(solution)/shard_map/reduce_scatter | solution.py:77
Async XLA Ops:
  6.5 136.9 %reduce-scatter.2.cloned.1.call-start = ((), (), s32[]{:S(2)}) async-start(), calls=%async_computation.1 | async-start | bytes 6291456 | tf_op jit(solution)/shard_map/reduce_scatter | solution.py:77
  6.5 48.8 %collective-permute-start = (bf16[256,4096]{1,0:T(8,128)(2,1)}, bf16[256,4096]{1,0:T(8,128)(2,1)S(1)}, u32[]{:S(2)}, u32[]{:S(2)}) collective-permute-start(bf16[256,4096]{1,0:T(8,128)(2,1)} %param.4), channel_id=1, source_target_pairs={{0,1},{1,0},{2,3},{3,2},{4,5},{5,4},{6,7},{7,6},{8,9},{9,8},{10,11... | collective-permute-start | bytes 6291464 | tf_op jit(solution)/shard_map/ppermute | solution.py:18
Sparse Core Ops, SparseCore 0:
  87.6 55.8 reduce-scatter.1
